TPU v7x, 128 devices: a whole 4x4x4 slice. The times are simulated.
128 devices in a mesh: shard: 32 (over y, z, core), rep: 4 (over x).
Axes of the slice: x: 4, y: 4, z: 4, core: 2. Of those that a mesh axis runs over, the one named last changes fastest.
Arguments:
- feats: bfloat16 [32768, 768], P('shard'), may hold values from -6 to 6
- bases: bfloat16 [4, 768, 1024], P(None, None, 'rep'), may hold values from -0.21875 to 0.21875
- coef: bfloat16 [5, 4], replicated, may hold values from -2 to 2
- root_weight: bfloat16 [768, 1024], P(None, 'rep'), may hold values from -0.21875 to 0.21875
- slot_block: int32 [32, 32, 2], P('shard'), may hold values from 0 to 7
- recv_rel: int32 [32, 32, 2], P('shard'), may hold values from 0 to 4
- tile_slot: int32 [32, 256], P('shard'), may hold values from 0 to 63, as said below
- tile_dst: int32 [32, 256], P('shard'), may hold values from 0 to 7
- tile_adj: bfloat16 [32, 256, 128, 128], P('shard'), may hold values from 0 to 0.049804688
- d_out: bfloat16 [32768, 1024], P('shard', 'rep'), may hold values from -6 to 6
Outputs:
- output: bfloat16 [32768, 1024], P('shard', 'rep')
- grad_feats: bfloat16 [32768, 768], P(('shard', 'rep'))
- grad_bases: float32 [4, 768, 1024], P(None, 'shard', 'rep')
- grad_root: float32 [768, 1024], P('shard', 'rep')
- grad_coef: float32 [5, 4], replicated
Inputs may be any that keep to these rules, and one draw needn't show every extreme that they name: `tile_slot`: in each row (one destination device) every one of the 64 slots is named by at least one tile.
All inputs are finite; a program needn't handle non-finite values.
Results may differ from a plain program's by a relative error of at most 0.0062.
Values may be sent and summed in bfloat16 or wider, within the bound.
No kernel may reach another device: no remote copies, remote signals or barrier semaphores. Data moves between devices by JAX's collectives and lax.ppermute only.
A program may use at most 192 MiB of HBM per device.

v0:
```python
import jax
import jax.numpy as jnp
from jax import lax
from jax.sharding import PartitionSpec as P

BLK = 128
highest = lax.Precision.HIGHEST


def project_slots(source, weights):
    return jnp.einsum("snc,sco->sno", source, weights, preferred_element_type=jnp.float32).astype(
        jnp.bfloat16
    )


def body(
    feats, bases, coef, root_weight, slot_block, recv_rel, tile_slot, tile_dst, tile_adj, d_out
):
    shards = lax.axis_size("shard")
    nblocks = feats.shape[0] // BLK
    width_in = feats.shape[1]
    width_out = root_weight.shape[1]
    relations = coef.shape[0]
    capacity = slot_block.shape[2]
    slot_count = shards * capacity
    rel_weights = (
        jnp.dot(coef, bases.reshape(bases.shape[0], -1), preferred_element_type=jnp.float32)
        .astype(jnp.bfloat16)
        .reshape(relations, width_in, width_out)
    )
    feat_blocks = feats.reshape(nblocks, BLK, width_in)
    send_block = slot_block[0]
    local_rel = recv_rel[0]
    owner_rel = lax.all_to_all(local_rel, "shard", split_axis=0, concat_axis=0, tiled=True)
    tile_ids = tile_slot[0]
    dest_ids = tile_dst[0]
    adjacency = tile_adj[0]
    root_term = jnp.dot(feats, root_weight, preferred_element_type=jnp.float32)
    slot_weights = rel_weights[local_rel.reshape(-1)]
    outgoing = feat_blocks[send_block]
    incoming = lax.all_to_all(outgoing, "shard", split_axis=0, concat_axis=0, tiled=True)
    slot_msgs = project_slots(incoming.reshape(slot_count, BLK, width_in), slot_weights)
    tile_msgs = slot_msgs[tile_ids]
    weighted = jnp.einsum("tij,tjo->tio", adjacency, tile_msgs, preferred_element_type=jnp.float32)
    dst_onehot = (dest_ids[:, None] == jnp.arange(nblocks)[None, :]).astype(jnp.float32)
    neighbor_sum = jnp.einsum("tb,tio->bio", dst_onehot, weighted, precision=highest).reshape(
        -1, width_out
    )
    output = (neighbor_sum + root_term).astype(jnp.bfloat16)
    grad_rows = d_out.reshape(nblocks, BLK, width_out)[dest_ids]
    tile_grads = jnp.einsum(
        "tji,tjo->tio", adjacency, grad_rows, preferred_element_type=jnp.float32
    )
    slot_onehot = (tile_ids[:, None] == jnp.arange(slot_count)[None, :]).astype(jnp.float32)
    slot_grads = jnp.einsum("ts,tio->sio", slot_onehot, tile_grads, precision=highest).astype(
        jnp.bfloat16
    )
    slot_grads = slot_grads.reshape(shards, capacity, BLK, width_out)
    returned = lax.all_to_all(slot_grads, "shard", split_axis=0, concat_axis=0, tiled=True)
    owner_key = (owner_rel * nblocks + send_block).reshape(-1)
    owner_onehot = (owner_key[:, None] == jnp.arange(relations * nblocks)[None, :]).astype(
        jnp.bfloat16
    )
    source_grads = jnp.einsum(
        "sk,sio->kio",
        owner_onehot,
        returned.reshape(slot_count, BLK, width_out),
        preferred_element_type=jnp.float32,
    )
    source_grads = source_grads.astype(jnp.bfloat16).reshape(relations, nblocks * BLK, width_out)
    through_rel = jnp.einsum(
        "rno,rco->nc", source_grads, rel_weights, preferred_element_type=jnp.float32
    )
    feature_sum = lax.psum_scatter(
        through_rel + jnp.dot(d_out, root_weight.T, preferred_element_type=jnp.float32),
        "rep",
        scatter_dimension=0,
        tiled=True,
    )
    grad_feats = feature_sum.astype(jnp.bfloat16)
    relation_grads = jnp.einsum(
        "nc,rno->cro", feats, source_grads, preferred_element_type=jnp.float32
    )
    root_grad = jnp.dot(feats.T, d_out, preferred_element_type=jnp.float32)
    stacked = jnp.concatenate([relation_grads, root_grad[:, None, :]], axis=1)
    reduced = lax.psum_scatter(stacked, "shard", scatter_dimension=0, tiled=True)
    grad_bases = jnp.einsum(
        "rb,iro->bio", coef.astype(jnp.float32), reduced[:, :relations], precision=highest
    )
    grad_root = reduced[:, relations]
    row_count = reduced.shape[0]
    base_rows = lax.dynamic_slice_in_dim(bases, lax.axis_index("shard") * row_count, row_count, 1)
    partial_coef = jnp.einsum(
        "iro,bio->rb", reduced[:, :relations], base_rows.astype(jnp.float32), precision=highest
    )
    grad_coef = lax.psum(partial_coef, ("shard", "rep"))
    return (output, grad_feats, grad_bases, grad_root, grad_coef)


def solution(mesh):
    placed = (
        P("shard", None),
        P(None, None, "rep"),
        P(),
        P(None, "rep"),
        P("shard", None, None),
        P("shard", None, None),
        P("shard", None),
        P("shard", None),
        P("shard", None, None, None),
        P("shard", "rep"),
    )
    return jax.shard_map(
        body,
        mesh=mesh,
        in_specs=placed,
        out_specs=(
            P("shard", "rep"),
            P(("shard", "rep"), None),
            P(None, "shard", "rep"),
            P("shard", "rep"),
            P(),
        ),
        check_vma=False,
    )
```

profile of v0, /device:TPU:1, one launch (start us, length us, event | category | flops | bytes accessed | tf_op | source)
XLA Modules:
  0.0 624.1 jit_solution(11586295730918086103)
XLA Ops:
  7.2 1.5 copy.60
  8.7 9.6 %all-to-all-start.1 = ((s32[32,1,2]{2,1,0:T(1,128)}), s32[32,1,2]{2,1,0:T(1,128)S(1)}, u32[]{:S(2)}, u32[]{:S(2)}) async-start(s32[32,1,2]{2,1,0:T(1,128)} %copy.60), calls=%async_computation.1 | async-start | bytes 32768 | tf_op jit(solution)/shard_map/all_to_all | solution.py:34
  18.3 0.7 compare_select_fusion
  19.0 10.8 %gather_fusion.3 = bf16[256,128,256]{2,1,0:T(8,128)(2,1)} fusion(bf16[8,128,256]{2,1,0:T(8,128)(2,1)} %bitcast.87, s32[1024]{0:T(1024)S(1)} %pad_clamp_fusion), kind=kCustom, calls=%fused_computation.3 | custom fusion | bytes 33555456 | tf_op jit(solution)/shard_map/gather | solution.py:50
  29.8 20.1 %convolution_bitcast_fusion = f32[256,128,256]{1,2,0:T(8,128)} fusion(bf16[256,128,256]{2,1,0:T(8,128)(2,1)} %gather_fusion.3, bf16[1,256,128,128]{3,2,1,0:T(8,128)(2,1)} %param.18), kind=kOutput, calls=%fused_computation.5 | convolution fusion | flops 2147483648 | bytes 58720256 | tf_op jit(solution)/shard_map/tji,tjo->tio/dot_general | solution.py:51
  49.9 33.4 %copy.63 = f32[256,128,256]{2,0,1:T(8,128)} copy(f32[256,128,256]{1,2,0:T(8,128)} %convolution_bitcast_fusion) | data formatting | bytes 67108864 | tf_op jit(solution)/shard_map/tji,tjo->tio/dot_general | solution.py:51
  83.3 19.2 %convolution_convert_fusion.1 = bf16[64,128,256]{2,0,1:T(8,128)(2,1)} fusion(f32[256,128,256]{2,0,1:T(8,128)} %copy.63, s32[256]{0:T(256)S(1)} %bitcast.99), kind=kOutput, calls=%fused_computation.11 | convolution fusion | flops 6444564480 | bytes 37749760 | tf_op jit(solution)/shard_map/ts,tio->sio/dot_general | solution.py:55
  102.4 7.2 %reshape.172 = bf16[32,2,128,256]{3,1,0,2:T(2,128)(2,1)} reshape(bf16[64,128,256]{2,0,1:T(8,128)(2,1)} %convolution_convert_fusion.1) | data formatting | bytes 8388608 | tf_op jit(solution)/shard_map/reshape | solution.py:58
  109.7 8.5 %copy.64 = bf16[32,2,128,256]{3,1,2,0:T(2,128)(2,1)} copy(bf16[32,2,128,256]{3,1,0,2:T(2,128)(2,1)} %reshape.172) | data formatting | bytes 8388608 | tf_op jit(solution)/shard_map/reshape | solution.py:58
  118.2 7.6 %all-to-all-start.2 = ((bf16[32,2,128,256]{3,1,2,0:T(2,128)(2,1)}), bf16[32,2,128,256]{3,1,2,0:T(2,128)(2,1)}, u32[]{:S(2)}, u32[]{:S(2)}) async-start(bf16[32,2,128,256]{3,1,2,0:T(2,128)(2,1)} %copy.64), calls=%async_computation.2 | async-start | bytes 8388608 | tf_op jit(solution)/shard_map/all_to_all | solution.py:59
  125.8 11.4 %reduce-scatter.5.cloned.1.call-start = ((), (), s32[]{:S(2)}) async-start(), calls=%async_computation.6 | async-start | bytes 6488064 | tf_op jit(solution)/shard_map/reduce_scatter | solution.py:86
  137.4 0.6 convolution_bitcast_fusion.3
  138.2 39.7 %all-to-all-done.2 = bf16[32,2,128,256]{3,1,2,0:T(2,128)(2,1)} async-done(((bf16[32,2,128,256]{3,1,2,0:T(2,128)(2,1)}), bf16[32,2,128,256]{3,1,2,0:T(2,128)(2,1)}, u32[]{:S(2)}, u32[]{:S(2)}) %all-to-all-start.2) | async-done | bytes 4194336 | tf_op jit(solution)/shard_map/all_to_all | solution.py:59
  178.0 8.9 %copy.65 = bf16[32,2,128,256]{3,1,0,2:T(2,128)(2,1)} copy(bf16[32,2,128,256]{3,1,2,0:T(2,128)(2,1)} %all-to-all-done.2) | data formatting | bytes 8388608 | tf_op jit(solution)/shard_map/all_to_all | solution.py:59
  186.9 7.2 %reshape.173 = bf16[64,128,256]{2,0,1:T(8,128)(2,1)} reshape(bf16[32,2,128,256]{3,1,0,2:T(2,128)(2,1)} %copy.65) | data formatting | bytes 8388608 | tf_op jit(solution)/shard_map/reshape | solution.py:67
  194.1 3.0 convolution_convert_fusion.3
  197.1 0.6 copy.66
  197.7 2.3 convolution_bitcast_fusion.2
  200.0 2.6 pad_maximum_fusion
  202.6 6.3 %copy.69 = f32[768,6,256]{2,1,0:T(8,128)} copy(f32[768,6,256]{0,2,1:T(8,128)} %pad_maximum_fusion) | data formatting | bytes 9437184 | tf_op jit(solution)/shard_map/concatenate | solution.py:85
  209.1 7.2 %gather_fusion = bf16[64,128,768]{2,1,0:T(8,128)(2,1)} fusion(bf16[8,128,768]{2,1,0:T(8,128)(2,1)S(1)} %bitcast.86, s32[1024]{0:T(1024)S(1)} %pad_clamp_fusion.3), kind=kCustom, calls=%fused_computation | custom fusion | bytes 25166080 | tf_op jit(solution)/shard_map/gather | solution.py:40
  216.3 7.3 %all-to-all-start = ((bf16[32,2,128,768]{3,2,1,0:T(8,128)(2,1)}), bf16[32,2,128,768]{3,2,1,0:T(8,128)(2,1)}, u32[]{:S(2)}, u32[]{:S(2)}) async-start(bf16[32,2,128,768]{3,2,1,0:T(8,128)(2,1)} %bitcast.90), calls=%async_computation | async-start | bytes 25165824 | tf_op jit(solution)/shard_map/all_to_all | solution.py:41
  223.7 2.7 copy.78
  226.4 1.3 convolution_convert_fusion
  227.7 0.4 copy.84
  228.2 2.2 fusion.19
  230.5 2.3 bitcast_add_fusion
  232.8 0.9 copy.56
  233.7 0.6 reshape_squeeze.3
  234.3 0.7 fusion.18
  235.0 11.0 %gather_fusion.1 = bf16[64,768,256]{2,1,0:T(8,128)(2,1)} fusion(bf16[5,768,256]{2,1,0:T(8,128)(2,1)S(1)} %bitcast.89, s32[1024]{0:T(1024)S(1)} %pad_clamp_fusion.2), kind=kCustom, calls=%fused_computation.1 | custom fusion | bytes 50331904 | tf_op jit(solution)/shard_map/gather | solution.py:39
  246.0 0.8 constant_dynamic-slice_fusion
  246.8 159.7 %reduce-scatter.5.cloned.1.call-done = f32[24,6,256]{2,1,0:T(8,128)} async-done(((f32[768,6,256]{2,1,0:T(8,128)}), f32[24,6,256]{2,1,0:T(8,128)}) %reduce-scatter.5.cloned.1.call-update) | async-done | bytes 147472 | tf_op jit(solution)/shard_map/reduce_scatter | solution.py:86
  406.5 1.2 convolution_bitcast_fusion.5
  407.7 40.2 %reduce-scatter.3.cloned.1.call-done = f32[256,768]{1,0:T(8,128)} async-done(((f32[1024,768]{1,0:T(8,128)}), f32[256,768]{1,0:T(8,128)}) %reduce-scatter.3.cloned.1.call-update) | async-done | bytes 786448 | tf_op jit(solution)/shard_map/reduce_scatter | solution.py:74
  447.9 1.9 convert_element_type.28
  449.9 64.9 %psum.7 = f32[5,4]{0,1:T(4,128)} all-reduce(f32[5,4]{0,1:T(4,128)S(1)} %convolution_bitcast_fusion.5), channel_id=1, replica_groups=mesh['shard'=32,'rep'=4] {'shard','rep'}, use_global_device_ids=true, to_apply=%region_2.0 | all-reduce | flops 20 | bytes 160 | tf_op jit(solution)/shard_map/psum | solution.py:96
  514.8 1.1 convolution_bitcast_fusion.4
  515.9 0.7 copy.71
  516.6 1.0 slice.18
  517.5 0.6 copy.85
  518.1 15.7 %convolution_convert_fusion.2 = bf16[64,128,256]{2,1,0:T(8,128)(2,1)} fusion(bf16[64,128,768]{2,1,0:T(8,128)(2,1)} %bitcast.5, bf16[64,768,256]{2,1,0:T(8,128)(2,1)} %gather_fusion.1), kind=kOutput, calls=%fused_computation.12 | convolution fusion | flops 3223322624 | bytes 41943040 | tf_op jit(solution)/shard_map/snc,sco->sno/dot_general | solution.py:11
  533.9 12.0 %gather_fusion.2 = bf16[256,128,256]{2,1,0:T(8,128)(2,1)} fusion(bf16[64,128,256]{2,1,0:T(8,128)(2,1)} %convolution_convert_fusion.2, s32[1024]{0:T(1024)S(1)} %pad_clamp_fusion.1), kind=kCustom, calls=%fused_computation.2 | custom fusion | bytes 33555456 | tf_op jit(solution)/shard_map/gather | solution.py:43
  545.9 20.1 %convolution_bitcast_fusion.1 = f32[256,128,256]{1,2,0:T(8,128)} fusion(bf16[256,128,256]{2,1,0:T(8,128)(2,1)} %gather_fusion.2, bf16[1,256,128,128]{3,2,1,0:T(8,128)(2,1)} %param.18), kind=kOutput, calls=%fused_computation.6 | convolution fusion | flops 2147483648 | bytes 58720256 | tf_op jit(solution)/shard_map/tij,tjo->tio/dot_general | solution.py:44
  566.0 33.4 %copy.58 = f32[256,128,256]{2,0,1:T(8,128)} copy(f32[256,128,256]{1,2,0:T(8,128)} %convolution_bitcast_fusion.1) | data formatting | bytes 67108864 | tf_op jit(solution)/shard_map/tij,tjo->tio/dot_general | solution.py:44
  599.4 15.8 %fusion.14 = f32[8,128,256]{2,0,1:T(8,128)S(1)} fusion(f32[256,128,256]{2,0,1:T(8,128)} %copy.58, s32[256]{0:T(256)S(1)} %bitcast.98), kind=kOutput, calls=%fused_computation.35 | convolution fusion | flops 805308416 | bytes 34604032 | tf_op jit(solution)/shard_map/tb,tio->bio/dot_general | solution.py:46
  615.2 0.3 copy.59
  615.5 1.4 fusion.3
  (46 shorter events, 0.7 us)
Async XLA Ops:
  7.2 130.3 %copy-start = (bf16[1024,768]{1,0:T(8,128)(2,1)S(1)}, bf16[1024,768]{1,0:T(8,128)(2,1)}, u32[]{:S(2)}) copy-start(bf16[1024,768]{1,0:T(8,128)(2,1)} %param.10) | copy-start | bytes 4718596
  8.7 109.5 %all-to-all-start.1 = ((s32[32,1,2]{2,1,0:T(1,128)}), s32[32,1,2]{2,1,0:T(1,128)S(1)}, u32[]{:S(2)}, u32[]{:S(2)}) async-start(s32[32,1,2]{2,1,0:T(1,128)} %copy.60), calls=%async_computation.1 | async-start | bytes 32768 | tf_op jit(solution)/shard_map/all_to_all | solution.py:34
  49.9 33.4 %copy-start.9 = (s32[1,256]{1,0:T(1,128)S(1)}, s32[1,256]{1,0:T(1,128)}, u32[]{:S(2)}) copy-start(s32[1,256]{1,0:T(1,128)} %param.16) | copy-start | bytes 3076
  118.2 19.0 %copy-start.11 = (s32[1,32,2]{1,2,0:T(2,128)S(1)}, s32[1,32,2]{1,2,0:T(2,128)}, u32[]{:S(2)}) copy-start(s32[1,32,2]{1,2,0:T(2,128)} %param.14) | copy-start | bytes 772
  118.2 19.2 %copy-start.1 = (bf16[1024,256]{1,0:T(8,128)(2,1)S(1)}, bf16[1024,256]{1,0:T(8,128)(2,1)}, u32[]{:S(2)}) copy-start(bf16[1024,256]{1,0:T(8,128)(2,1)} %param.19) | copy-start | bytes 1572868
  118.2 59.8 %all-to-all-start.2 = ((bf16[32,2,128,256]{3,1,2,0:T(2,128)(2,1)}), bf16[32,2,128,256]{3,1,2,0:T(2,128)(2,1)}, u32[]{:S(2)}, u32[]{:S(2)}) async-start(bf16[32,2,128,256]{3,1,2,0:T(2,128)(2,1)} %copy.64), calls=%async_computation.2 | async-start | bytes 8388608 | tf_op jit(solution)/shard_map/all_to_all | solution.py:59
  125.8 280.7 %reduce-scatter.5.cloned.1.call-start = ((), (), s32[]{:S(2)}) async-start(), calls=%async_computation.6 | async-start | bytes 6488064 | tf_op jit(solution)/shard_map/reduce_scatter | solution.py:86
  197.7 2.3 copy-start.4
  216.3 10.0 %copy-start.12 = (bf16[5,4]{0,1:T(4,128)(2,1)S(1)}, bf16[5,4]{0,1:T(4,128)(2,1)}, u32[]{:S(2)}) copy-start(bf16[5,4]{0,1:T(4,128)(2,1)} %param.12) | copy-start | bytes 124
  216.3 301.8 %all-to-all-start = ((bf16[32,2,128,768]{3,2,1,0:T(8,128)(2,1)}), bf16[32,2,128,768]{3,2,1,0:T(8,128)(2,1)}, u32[]{:S(2)}, u32[]{:S(2)}) async-start(bf16[32,2,128,768]{3,2,1,0:T(8,128)(2,1)} %bitcast.90), calls=%async_computation | async-start | bytes 25165824 | tf_op jit(solution)/shard_map/all_to_all | solution.py:41
  223.6 224.3 %reduce-scatter.3.cloned.1.call-start = ((), (), s32[]{:S(2)}) async-start(), calls=%async_computation.5 | async-start | bytes 3932160 | tf_op jit(solution)/shard_map/reduce_scatter | solution.py:74
  226.4 1.8 copy-start.5
  228.2 2.3 copy-start.2
  228.2 2.2 copy-start.6
  232.8 2.2 copy-start.3
  235.0 11.0 %copy-start.10 = (s32[1,256]{1,0:T(1,128)S(1)}, s32[1,256]{1,0:T(1,128)}, u32[]{:S(2)}) copy-start(s32[1,256]{1,0:T(1,128)} %param.16) | copy-start | bytes 3076
  235.0 279.8 %copy-start.13 = (bf16[5,4]{0,1:T(4,128)(2,1)S(1)}, bf16[5,4]{0,1:T(4,128)(2,1)}, u32[]{:S(2)}) copy-start(bf16[5,4]{0,1:T(4,128)(2,1)} %param.12) | copy-start | bytes 124
  566.0 33.4 %copy-start.8 = (s32[1,256]{1,0:T(1,128)S(1)}, s32[1,256]{1,0:T(1,128)}, u32[]{:S(2)}) copy-start(s32[1,256]{1,0:T(1,128)} %param.17) | copy-start | bytes 3076
  599.4 16.1 %copy-start.7 = (bf16[768,256]{1,0:T(8,128)(2,1)S(1)}, bf16[768,256]{1,0:T(8,128)(2,1)}, u32[]{:S(2)}) copy-start(bf16[768,256]{1,0:T(8,128)(2,1)} %param.13) | copy-start | bytes 1179652
Sparse Core Ops, SparseCore 0:
  209.0 197.4 reduce-scatter.4
  409.0 38.8 reduce-scatter.2
where the time goes:
time: 635 us; the launch traced here: 624 us
  waiting for transfers between devices  240 us (38%)
  local copies, waits for them, and re-layouts  157 us (25%)
  matrix products  106 us (17%)
  blocking collectives  64.9 us (10%)
  starting transfers between devices  35.9 us (6%)
  between operations  14.7 us (2%)
    reduce_scatter x1, waiting for transfers between devices, body(): lax.psum_scatter(stacked, 'shard', scatter_dimension=0, tiled=True)  160 us
    psum x1, blocking collectives, body(): grad_coef = lax.psum(partial_coef, ('shard', 'rep'))  64.9 us
    reduce_scatter x1, waiting for transfers between devices, body(): lax.psum_scatter(through_rel + jnp.dot(d_out, root_weight.T, preferred_el...  40.2 us
    all_to_all x1, waiting for transfers between devices, body(): lax.all_to_all(slot_grads, 'shard', split_axis=0, concat_axis=0, tiled=True)  39.7 us
    dot_general x1, local copies, waits for them, and re-layouts, body(): jnp.einsum('tij,tjo->tio', adjacency, tile_msgs, preferred_element_type=j...  33.4 us
    dot_general x1, local copies, waits for them, and re-layouts, body(): jnp.einsum('tji,tjo->tio', adjacency, grad_rows, preferred_element_type=j...  33.4 us
    dot_general x1, matrix products, body(): jnp.einsum('tij,tjo->tio', adjacency, tile_msgs, preferred_element_type=j...  20.1 us
    dot_general x1, matrix products, body(): jnp.einsum('tji,tjo->tio', adjacency, grad_rows, preferred_element_type=j...  20.1 us
  transfers between devices with their start and end apart: 5, of which 3 were waited for; matrix products, arithmetic and copies ran while one was open for 22% of the time, Pallas kernels for 0%

commit v1 on v0

--- a/solution.py
+++ b/solution.py
@@ -5,6 +5,12 @@
 
 BLK = 128
 highest = lax.Precision.HIGHEST
+
+
+def gather_and_add(x, axis):
+    terms = lax.all_gather(x, axis, axis=0, tiled=False)
+    summed = terms.sum(axis=0)
+    return summed
 
 
 def project_slots(source, weights):
@@ -93,7 +99,7 @@
     partial_coef = jnp.einsum(
         "iro,bio->rb", reduced[:, :relations], base_rows.astype(jnp.float32), precision=highest
     )
-    grad_coef = lax.psum(partial_coef, ("shard", "rep"))
+    grad_coef = gather_and_add(partial_coef, ("shard", "rep"))
     return (output, grad_feats, grad_bases, grad_root, grad_coef)
 
 

time: 635 us -> 594 us (0.935)
  waiting for transfers between devices: 240 us -> 202 us
  starting transfers between devices: 35.9 us -> 24.8 us
    all_gather x0 -> x1, blocking collectives: none -> 69.4 us  [gather_and_add(): terms = lax.all_gather(x, axis, axis=0, tiled=False)]
    psum x1 -> x0, blocking collectives: 64.9 us -> none  [body(): grad_coef = lax.psum(partial_coef, ('shard', 'rep'))]
    reduce_scatter x1, waiting for transfers between devices: 40.2 us -> 0.01 us  [body(): lax.psum_scatter(through_rel + jnp.dot(d_out, root_weight.T, preferred_el...]
    reduce_scatter x1, starting transfers between devices: 11.4 us -> 0.25 us  [body(): lax.psum_scatter(stacked, 'shard', scatter_dimension=0, tiled=True)]
    all_to_all x1, waiting for transfers between devices: 39.7 us -> 47.3 us  [body(): lax.all_to_all(slot_grads, 'shard', split_axis=0, concat_axis=0, tiled=True)]
  transfers between devices with their start and end apart: 5 -> 5, of which waited for: 3 -> 2; matrix products, arithmetic and copies ran while one was open for 22% -> 25% of each run, Pallas kernels for 0% -> 0%
where the time goes in v1:
time: 594 us; the launch traced here: 582 us
  waiting for transfers between devices  202 us (34%)
  local copies, waits for them, and re-layouts  156 us (26%)
  matrix products  108 us (18%)
  blocking collectives  69.4 us (12%)
  starting transfers between devices  24.8 us (4%)
  between operations  14.7 us (2%)
  other arithmetic  6.76 us (1%)
    reduce_scatter x1, waiting for transfers between devices, body(): lax.psum_scatter(stacked, 'shard', scatter_dimension=0, tiled=True)  155 us
    all_gather x1, blocking collectives, gather_and_add(): terms = lax.all_gather(x, axis, axis=0, tiled=False)  69.4 us
    all_to_all x1, waiting for transfers between devices, body(): lax.all_to_all(slot_grads, 'shard', split_axis=0, concat_axis=0, tiled=True)  47.3 us
    dot_general x1, local copies, waits for them, and re-layouts, body(): jnp.einsum('tji,tjo->tio', adjacency, grad_rows, preferred_element_type=j...  33.4 us
    dot_general x1, local copies, waits for them, and re-layouts, body(): jnp.einsum('tij,tjo->tio', adjacency, tile_msgs, preferred_element_type=j...  33.4 us
    dot_general x1, matrix products, body(): jnp.einsum('tij,tjo->tio', adjacency, tile_msgs, preferred_element_type=j...  20.1 us
    dot_general x1, matrix products, body(): jnp.einsum('tji,tjo->tio', adjacency, grad_rows, preferred_element_type=j...  20.1 us
    dot_general x1, matrix products, body(): jnp.einsum('ts,tio->sio', slot_onehot, tile_grads, precision=highest)  19.2 us
  transfers between devices with their start and end apart: 5, of which 2 were waited for; matrix products, arithmetic and copies ran while one was open for 25% of the time, Pallas kernels for 0%

profile of v1, /device:TPU:1, one launch (start us, length us, event | category | flops | bytes accessed | tf_op | source)
XLA Modules:
  0.0 581.9 jit_solution(5979839053594988120)
XLA Ops:
  7.2 1.5 copy.60
  8.7 9.6 %all-to-all-start.1 = ((s32[32,1,2]{2,1,0:T(1,128)}), s32[32,1,2]{2,1,0:T(1,128)S(1)}, u32[]{:S(2)}, u32[]{:S(2)}) async-start(s32[32,1,2]{2,1,0:T(1,128)} %copy.60), calls=%async_computation.1 | async-start | bytes 32768 | tf_op jit(solution)/shard_map/all_to_all | solution.py:40
  18.3 0.7 compare_select_fusion
  19.0 10.8 %gather_fusion.3 = bf16[256,128,256]{2,1,0:T(8,128)(2,1)} fusion(bf16[8,128,256]{2,1,0:T(8,128)(2,1)} %bitcast.88, s32[1024]{0:T(1024)S(1)} %pad_clamp_fusion), kind=kCustom, calls=%fused_computation.3 | custom fusion | bytes 33555456 | tf_op jit(solution)/shard_map/gather | solution.py:56
  29.8 20.1 %convolution_bitcast_fusion = f32[256,128,256]{1,2,0:T(8,128)} fusion(bf16[256,128,256]{2,1,0:T(8,128)(2,1)} %gather_fusion.3, bf16[1,256,128,128]{3,2,1,0:T(8,128)(2,1)} %param.18), kind=kOutput, calls=%fused_computation.5 | convolution fusion | flops 2147483648 | bytes 58720256 | tf_op jit(solution)/shard_map/tji,tjo->tio/dot_general | solution.py:57
  49.9 33.4 %copy.63 = f32[256,128,256]{2,0,1:T(8,128)} copy(f32[256,128,256]{1,2,0:T(8,128)} %convolution_bitcast_fusion) | data formatting | bytes 67108864 | tf_op jit(solution)/shard_map/tji,tjo->tio/dot_general | solution.py:57
  83.3 19.2 %convolution_convert_fusion.1 = bf16[64,128,256]{2,0,1:T(8,128)(2,1)} fusion(f32[256,128,256]{2,0,1:T(8,128)} %copy.63, s32[256]{0:T(256)S(1)} %bitcast.100), kind=kOutput, calls=%fused_computation.11 | convolution fusion | flops 6444564480 | bytes 37749760 | tf_op jit(solution)/shard_map/ts,tio->sio/dot_general | solution.py:61
  102.4 7.2 %reshape.172 = bf16[32,2,128,256]{3,1,0,2:T(2,128)(2,1)} reshape(bf16[64,128,256]{2,0,1:T(8,128)(2,1)} %convolution_convert_fusion.1) | data formatting | bytes 8388608 | tf_op jit(solution)/shard_map/reshape | solution.py:64
  109.6 8.5 %copy.64 = bf16[32,2,128,256]{3,1,2,0:T(2,128)(2,1)} copy(bf16[32,2,128,256]{3,1,0,2:T(2,128)(2,1)} %reshape.172) | data formatting | bytes 8388608 | tf_op jit(solution)/shard_map/reshape | solution.py:64
  118.1 7.6 %all-to-all-start.2 = ((bf16[32,2,128,256]{3,1,2,0:T(2,128)(2,1)}), bf16[32,2,128,256]{3,1,2,0:T(2,128)(2,1)}, u32[]{:S(2)}, u32[]{:S(2)}) async-start(bf16[32,2,128,256]{3,1,2,0:T(2,128)(2,1)} %copy.64), calls=%async_computation.2 | async-start | bytes 8388608 | tf_op jit(solution)/shard_map/all_to_all | solution.py:65
  126.1 1.2 copy.78
  127.4 1.3 convolution_convert_fusion
  128.7 1.8 copy.84
  130.6 47.3 %all-to-all-done.2 = bf16[32,2,128,256]{3,1,2,0:T(2,128)(2,1)} async-done(((bf16[32,2,128,256]{3,1,2,0:T(2,128)(2,1)}), bf16[32,2,128,256]{3,1,2,0:T(2,128)(2,1)}, u32[]{:S(2)}, u32[]{:S(2)}) %all-to-all-start.2) | async-done | bytes 4194336 | tf_op jit(solution)/shard_map/all_to_all | solution.py:65
  177.9 8.9 %copy.65 = bf16[32,2,128,256]{3,1,0,2:T(2,128)(2,1)} copy(bf16[32,2,128,256]{3,1,2,0:T(2,128)(2,1)} %all-to-all-done.2) | data formatting | bytes 8388608 | tf_op jit(solution)/shard_map/all_to_all | solution.py:65
  186.8 7.2 %reshape.173 = bf16[64,128,256]{2,0,1:T(8,128)(2,1)} reshape(bf16[32,2,128,256]{3,1,0,2:T(2,128)(2,1)} %copy.65) | data formatting | bytes 8388608 | tf_op jit(solution)/shard_map/reshape | solution.py:73
  194.0 3.2 convolution_convert_fusion.3
  197.2 0.6 copy.66
  197.8 2.2 fusion.19
  200.1 2.3 bitcast_add_fusion
  202.7 7.2 %gather_fusion = bf16[64,128,768]{2,1,0:T(8,128)(2,1)} fusion(bf16[8,128,768]{2,1,0:T(8,128)(2,1)S(1)} %bitcast.87, s32[1024]{0:T(1024)S(1)} %pad_clamp_fusion.3), kind=kCustom, calls=%fused_computation | custom fusion | bytes 25166080 | tf_op jit(solution)/shard_map/gather | solution.py:46
  209.9 7.1 %all-to-all-start = ((bf16[32,2,128,768]{3,2,1,0:T(8,128)(2,1)}), bf16[32,2,128,768]{3,2,1,0:T(8,128)(2,1)}, u32[]{:S(2)}, u32[]{:S(2)}) async-start(bf16[32,2,128,768]{3,2,1,0:T(8,128)(2,1)} %bitcast.91), calls=%async_computation | async-start | bytes 25165824 | tf_op jit(solution)/shard_map/all_to_all | solution.py:47
  217.1 0.3 reduce-scatter.5.cloned.1.call-start
  217.3 0.6 convolution_bitcast_fusion.3
  217.9 4.0 convolution_bitcast_fusion.2
  222.0 2.7 pad_maximum_fusion
  224.7 6.3 %copy.69 = f32[768,6,256]{2,1,0:T(8,128)} copy(f32[768,6,256]{0,2,1:T(8,128)} %pad_maximum_fusion) | data formatting | bytes 9437184 | tf_op jit(solution)/shard_map/concatenate | solution.py:91
  231.0 0.9 copy.56
  231.9 0.6 reshape_squeeze.3
  232.6 0.7 fusion.18
  233.2 10.5 %gather_fusion.1 = bf16[64,768,256]{2,1,0:T(8,128)(2,1)} fusion(bf16[5,768,256]{2,1,0:T(8,128)(2,1)S(1)} %bitcast.90, s32[1024]{0:T(1024)S(1)} %pad_clamp_fusion.2), kind=kCustom, calls=%fused_computation.1 | custom fusion | bytes 50331904 | tf_op jit(solution)/shard_map/gather | solution.py:45
  243.7 0.8 constant_dynamic-slice_fusion
  244.6 1.9 convert_element_type.28
  246.5 154.7 %reduce-scatter.5.cloned.1.call-done = f32[24,6,256]{2,1,0:T(8,128)} async-done(((f32[768,6,256]{2,1,0:T(8,128)}), f32[24,6,256]{2,1,0:T(8,128)}) %reduce-scatter.5.cloned.1.call-update) | async-done | bytes 147472 | tf_op jit(solution)/shard_map/reduce_scatter | solution.py:92
  401.2 1.1 convolution_bitcast_fusion.4
  402.4 0.7 copy.71
  403.0 1.0 slice.18
  404.0 0.6 copy.85
  404.6 1.2 convolution_bitcast_fusion.5
  405.8 69.4 %all-gather.1 = f32[128,5,4]{1,2,0:T(4,128)S(1)} all-gather(f32[1,5,4]{1,2,0:T(4,128)S(1)} %convolution_bitcast_fusion.5), channel_id=2, replica_groups=mesh['shard'=32,'rep'=4] {'shard','rep'}, dimensions={0}, use_global_device_ids=true | all-gather | bytes 10320 | tf_op jit(solution)/shard_map/all_gather | solution.py:11
  475.2 0.7 reduce_sum.9
  476.0 15.7 %convolution_convert_fusion.2 = bf16[64,128,256]{2,1,0:T(8,128)(2,1)} fusion(bf16[64,128,768]{2,1,0:T(8,128)(2,1)} %bitcast.5, bf16[64,768,256]{2,1,0:T(8,128)(2,1)} %gather_fusion.1), kind=kOutput, calls=%fused_computation.12 | convolution fusion | flops 3223322624 | bytes 41943040 | tf_op jit(solution)/shard_map/snc,sco->sno/dot_general | solution.py:17
  491.7 12.0 %gather_fusion.2 = bf16[256,128,256]{2,1,0:T(8,128)(2,1)} fusion(bf16[64,128,256]{2,1,0:T(8,128)(2,1)} %convolution_convert_fusion.2, s32[1024]{0:T(1024)S(1)} %pad_clamp_fusion.1), kind=kCustom, calls=%fused_computation.2 | custom fusion | bytes 33555456 | tf_op jit(solution)/shard_map/gather | solution.py:49
  503.7 20.1 %convolution_bitcast_fusion.1 = f32[256,128,256]{1,2,0:T(8,128)} fusion(bf16[256,128,256]{2,1,0:T(8,128)(2,1)} %gather_fusion.2, bf16[1,256,128,128]{3,2,1,0:T(8,128)(2,1)} %param.18), kind=kOutput, calls=%fused_computation.6 | convolution fusion | flops 2147483648 | bytes 58720256 | tf_op jit(solution)/shard_map/tij,tjo->tio/dot_general | solution.py:50
  523.8 33.4 %copy.58 = f32[256,128,256]{2,0,1:T(8,128)} copy(f32[256,128,256]{1,2,0:T(8,128)} %convolution_bitcast_fusion.1) | data formatting | bytes 67108864 | tf_op jit(solution)/shard_map/tij,tjo->tio/dot_general | solution.py:50
  557.2 15.8 %fusion.14 = f32[8,128,256]{2,0,1:T(8,128)S(1)} fusion(f32[256,128,256]{2,0,1:T(8,128)} %copy.58, s32[256]{0:T(256)S(1)} %bitcast.99), kind=kOutput, calls=%fused_computation.35 | convolution fusion | flops 805308416 | bytes 34604032 | tf_op jit(solution)/shard_map/tb,tio->bio/dot_general | solution.py:52
  573.0 0.3 copy.59
  573.3 1.4 fusion.3
  (47 shorter events, 0.9 us)
Async XLA Ops:
  7.2 195.5 %copy-start = (bf16[1024,768]{1,0:T(8,128)(2,1)S(1)}, bf16[1024,768]{1,0:T(8,128)(2,1)}, u32[]{:S(2)}) copy-start(bf16[1024,768]{1,0:T(8,128)(2,1)} %param.10) | copy-start | bytes 4718596
  8.7 109.5 %all-to-all-start.1 = ((s32[32,1,2]{2,1,0:T(1,128)}), s32[32,1,2]{2,1,0:T(1,128)S(1)}, u32[]{:S(2)}, u32[]{:S(2)}) async-start(s32[32,1,2]{2,1,0:T(1,128)} %copy.60), calls=%async_computation.1 | async-start | bytes 32768 | tf_op jit(solution)/shard_map/all_to_all | solution.py:40
  49.9 33.4 %copy-start.9 = (s32[1,256]{1,0:T(1,128)S(1)}, s32[1,256]{1,0:T(1,128)}, u32[]{:S(2)}) copy-start(s32[1,256]{1,0:T(1,128)} %param.16) | copy-start | bytes 3076
  118.1 7.8 %copy-start.11 = (s32[1,32,2]{1,2,0:T(2,128)S(1)}, s32[1,32,2]{1,2,0:T(2,128)}, u32[]{:S(2)}) copy-start(s32[1,32,2]{1,2,0:T(2,128)} %param.14) | copy-start | bytes 772
  118.1 8.0 %copy-start.5 = (bf16[4,768,256]{2,1,0:T(8,128)(2,1)S(1)}, bf16[4,768,256]{2,1,0:T(8,128)(2,1)}, u32[]{:S(2)}) copy-start(bf16[4,768,256]{2,1,0:T(8,128)(2,1)} %param.11) | copy-start | bytes 4718596
  118.1 9.2 %copy-start.12 = (bf16[5,4]{0,1:T(4,128)(2,1)S(1)}, bf16[5,4]{0,1:T(4,128)(2,1)}, u32[]{:S(2)}) copy-start(bf16[5,4]{0,1:T(4,128)(2,1)} %param.12) | copy-start | bytes 124
  118.1 59.8 %all-to-all-start.2 = ((bf16[32,2,128,256]{3,1,2,0:T(2,128)(2,1)}), bf16[32,2,128,256]{3,1,2,0:T(2,128)(2,1)}, u32[]{:S(2)}, u32[]{:S(2)}) async-start(bf16[32,2,128,256]{3,1,2,0:T(2,128)(2,1)} %copy.64), calls=%async_computation.2 | async-start | bytes 8388608 | tf_op jit(solution)/shard_map/all_to_all | solution.py:65
  125.7 118.8 %reduce-scatter.3.cloned.1.call-start = ((), (), s32[]{:S(2)}) async-start(), calls=%async_computation.5 | async-start | bytes 3932160 | tf_op jit(solution)/shard_map/reduce_scatter | solution.py:80
  194.0 3.8 copy-start.2
  197.8 2.3 copy-start.4
  197.8 2.3 copy-start.1
  197.8 2.3 copy-start.6
  209.9 266.0 %all-to-all-start = ((bf16[32,2,128,768]{3,2,1,0:T(8,128)(2,1)}), bf16[32,2,128,768]{3,2,1,0:T(8,128)(2,1)}, u32[]{:S(2)}, u32[]{:S(2)}) async-start(bf16[32,2,128,768]{3,2,1,0:T(8,128)(2,1)} %bitcast.91), calls=%async_computation | async-start | bytes 25165824 | tf_op jit(solution)/shard_map/all_to_all | solution.py:47
  217.1 184.1 %reduce-scatter.5.cloned.1.call-start = ((), (), s32[]{:S(2)}) async-start(), calls=%async_computation.6 | async-start | bytes 6488064 | tf_op jit(solution)/shard_map/reduce_scatter | solution.py:92
  231.0 2.2 copy-start.3
  233.2 10.5 %copy-start.10 = (s32[1,256]{1,0:T(1,128)S(1)}, s32[1,256]{1,0:T(1,128)}, u32[]{:S(2)}) copy-start(s32[1,256]{1,0:T(1,128)} %param.16) | copy-start | bytes 3076
  233.2 168.0 %copy-start.13 = (bf16[5,4]{0,1:T(4,128)(2,1)S(1)}, bf16[5,4]{0,1:T(4,128)(2,1)}, u32[]{:S(2)}) copy-start(bf16[5,4]{0,1:T(4,128)(2,1)} %param.12) | copy-start | bytes 124
  523.8 33.4 %copy-start.8 = (s32[1,256]{1,0:T(1,128)S(1)}, s32[1,256]{1,0:T(1,128)}, u32[]{:S(2)}) copy-start(s32[1,256]{1,0:T(1,128)} %param.17) | copy-start | bytes 3076
  557.2 16.1 %copy-start.7 = (bf16[768,256]{1,0:T(8,128)(2,1)S(1)}, bf16[768,256]{1,0:T(8,128)(2,1)}, u32[]{:S(2)}) copy-start(bf16[768,256]{1,0:T(8,128)(2,1)} %param.13) | copy-start | bytes 1179652
Sparse Core Ops, SparseCore 0:
  202.6 38.9 reduce-scatter.2
  245.4 155.7 reduce-scatter.4
